TPU v7x, 32 devices: a whole 2x2x4 slice. The times are simulated.
32 devices in a mesh: docs: 8 (over z, x), topics: 4 (over y, core).
Axes of the slice: x: 2, y: 2, z: 4, core: 2. Of those that a mesh axis runs over, the one named last changes fastest.
Arguments:
- log_beta: bfloat16 [262144, 2048], P('docs', 'topics'), may hold values from -250 to -4
- gamma_init: float32 [128, 2048], P('docs', 'topics'), may hold values from 0.05 to 5
- topic_prior: float32 [2048], P('topics'), may hold values from 0.02 to 0.5
- word_block: int32 [128, 256, 1], P('docs'), may hold values from 0 to 7; in each aligned block of 4096 rows (0 to 4095, 4096 to 8191, ..., all dimensions but the last counted through in order) at most 1024 rows name the same one
- word_row: int32 [128, 256], P('docs'), may hold values from 0 to 32767
- counts: int32 [128, 256], P('docs'), may hold values from 0 to 2
Outputs:
- doc_gamma: float32 [128, 2048], P('docs', 'topics')
- sstats: float32 [262144, 2048], P('docs', 'topics')
Inputs may be any that keep to these rules, and one draw needn't show every extreme that they name: `word_block`: among the token slots of one device's 16 documents, at most 1024 name the same vocabulary block, and some block is named by exactly 1024 of them on some device. `counts`: A count of 0 marks an empty slot.
All inputs are finite; a program needn't handle non-finite values.
Results may differ from a plain program's by a relative error of at most 0.0003.
Values may be sent and summed in bfloat16 or wider, within the bound.
No kernel may reach another device: no remote copies, remote signals or barrier semaphores. Data moves between devices by JAX's collectives and lax.ppermute only.
A program may use at most 192 MiB of HBM per device.

v0:
```python
import jax
import jax.numpy as jnp
from jax import lax
from jax.sharding import PartitionSpec as P

ITERS = 3


def slot_places(word_owner, owners, capacity):
    length = word_owner.shape[1]
    member = (word_owner[:, None, :] == jnp.arange(owners, dtype=jnp.int32)[None, :, None]).astype(
        jnp.float32
    )
    earlier = (jnp.arange(length)[:, None] > jnp.arange(length)[None, :]).astype(jnp.float32)
    before = jnp.einsum("dom,nm->don", member, earlier, precision=lax.Precision.HIGHEST)
    per_doc = jnp.sum(member, axis=2)
    offset = jnp.cumsum(per_doc, axis=0) - per_doc
    slot_rank = jnp.sum(member * (before + offset[:, :, None]), axis=1)
    return word_owner * capacity + slot_rank.astype(jnp.int32)


def normalized(log_theta, token_rows):
    scores = log_theta[:, None, :] + token_rows.astype(jnp.float32)
    row_max = lax.pmax(jnp.max(scores, axis=2), "topics")
    exp_mass = lax.psum(jnp.sum(jnp.exp(scores - row_max[:, :, None]), axis=2), "topics")
    return (scores, row_max + jnp.log(exp_mass))


def per_device(log_beta, gamma_init, topic_prior, word_block, word_row, counts):
    doc_rows, length = counts.shape
    topic_cols = log_beta.shape[1]
    owners = lax.axis_size("docs")
    tokens = doc_rows * length
    capacity = 2 * tokens // owners
    weight = counts.astype(jnp.float32)
    places = slot_places(word_block[:, :, 0], owners, capacity).reshape(tokens)
    holder = jnp.arange(doc_rows, dtype=jnp.int32)[:, None] + jnp.zeros((1, length), jnp.int32)
    blank_ids = jnp.zeros((owners * capacity,), jnp.int32)
    requests = (
        blank_ids.at[places].set(word_row.reshape(tokens)).reshape(owners, capacity),
        blank_ids.at[places].set(holder.reshape(tokens)).reshape(owners, capacity),
        blank_ids.at[places].set(counts.reshape(tokens)).reshape(owners, capacity),
    )
    request = (
        lax.all_to_all(requests[0], "docs", split_axis=0, concat_axis=0, tiled=True),
        lax.all_to_all(requests[1], "docs", split_axis=0, concat_axis=0, tiled=True),
        lax.all_to_all(requests[2], "docs", split_axis=0, concat_axis=0, tiled=True),
    )
    found_rows = log_beta[request[0]]
    returned = lax.all_to_all(found_rows, "docs", split_axis=0, concat_axis=0, tiled=True)
    fetched, found_rows, own_rows, own_docs, own_counts = (
        returned,
        found_rows,
        request[0],
        request[1],
        request[2],
    )
    token_rows = fetched.reshape(owners * capacity, topic_cols)[places].reshape(
        doc_rows, length, topic_cols
    )
    doc_gamma = gamma_init
    for sweep_index in range(ITERS + 1):
        log_theta = lax.digamma(doc_gamma)
        scores, log_norm = normalized(log_theta, token_rows)
        topic_share = jnp.exp(scores - log_norm[:, :, None])
        if sweep_index < ITERS:
            doc_gamma = topic_prior[None, :] + jnp.einsum(
                "dn,dnk->dk", weight, topic_share, precision=lax.Precision.HIGHEST
            )
    theta_all = lax.all_gather(log_theta, "docs", axis=0, tiled=True)
    norm_slots = (
        jnp.zeros((owners * capacity,), jnp.float32)
        .at[places]
        .set(log_norm.reshape(tokens))
        .reshape(owners, capacity)
    )
    norm_back = lax.all_to_all(norm_slots, "docs", split_axis=0, concat_axis=0, tiled=True)
    source = jnp.arange(owners, dtype=jnp.int32)[:, None] * doc_rows + own_docs
    rescored = theta_all[source] + found_rows.astype(jnp.float32)
    stat_terms = own_counts.astype(jnp.float32)[:, :, None] * jnp.exp(
        rescored - norm_back[:, :, None]
    )
    sstats = (
        jnp.zeros((log_beta.shape[0], topic_cols), jnp.float32)
        .at[own_rows.reshape(-1)]
        .add(stat_terms.reshape(-1, topic_cols))
    )
    return (doc_gamma, sstats)


def solution(mesh):
    in_specs = (
        P("docs", "topics"),
        P("docs", "topics"),
        P("topics"),
        P("docs", None, None),
        P("docs", None),
        P("docs", None),
    )
    out_specs = (P("docs", "topics"), P("docs", "topics"))
    return jax.shard_map(
        per_device, mesh=mesh, in_specs=in_specs, out_specs=out_specs, check_vma=False
    )
```

profile of v0, /device:TPU:0, one launch (start us, length us, event | category | flops | bytes accessed | tf_op | source)
XLA Modules:
  0.0 973.2 jit_solution(9666026314543805726)
XLA Ops:
  3.3 16.1 %scatter_custom_fusion = s32[8192]{0:T(1024)} fusion(s32[4096]{0:T(1024)S(1)} %bitcast.87, s32[4096]{0:T(1024)S(1)} %bitcast.98, s32[]{:T(128)} %constant.30.clone.1), kind=kCustom, calls=%fused_computation.104 | custom fusion | bytes 32772 | tf_op jit(solution)/shard_map/scatter | solution.py:40
  19.4 7.3 all-to-all-start
  27.4 16.1 %scatter_custom_fusion.1 = s32[8192]{0:T(1024)} fusion(s32[4096]{0:T(1024)S(1)} %bitcast.88, s32[4096]{0:T(1024)S(1)} %bitcast.101, s32[]{:T(128)} %constant.30.clone.1), kind=kCustom, calls=%fused_computation.102 | custom fusion | bytes 32772 | tf_op jit(solution)/shard_map/scatter | solution.py:42
  43.5 16.1 %scatter_custom_fusion.2 = s32[8192]{0:T(1024)} fusion(s32[4096]{0:T(1024)S(1)} %bitcast.89, s32[4096]{0:T(1024)S(1)} %bitcast.99, s32[]{:T(128)} %constant.30.clone.1), kind=kCustom, calls=%fused_computation.100 | custom fusion | bytes 32772 | tf_op jit(solution)/shard_map/scatter | solution.py:41
  59.6 6.0 all-to-all-start.2
  65.6 6.6 all-to-all-done.2
  75.6 191.8 %gather_fusion = bf16[8192,512]{1,0:T(8,128)(2,1)} fusion(bf16[32768,512]{1,0:T(8,128)(2,1)} %param.6, s32[8192]{0:T(1024)S(1)} %broadcast_clamp_fusion.2), kind=kCustom, calls=%fused_computation | custom fusion | bytes 16809984 | tf_op jit(solution)/shard_map/gather | solution.py:49
  267.4 124.4 %all-to-all-start.1 = ((bf16[8,1024,512]{2,1,0:T(8,128)(2,1)}), bf16[8,1024,512]{2,1,0:T(8,128)(2,1)}, u32[]{:S(2)}, u32[]{:S(2)}) async-start(bf16[8,1024,512]{2,1,0:T(8,128)(2,1)} %bitcast.78), calls=%async_computation.1 | async-start | bytes 16777216 | tf_op jit(solution)/shard_map/all_to_all | solution.py:50
  392.1 5.9 sort
  398.2 176.0 %all-to-all-done.1 = bf16[8,1024,512]{2,1,0:T(8,128)(2,1)} async-done(((bf16[8,1024,512]{2,1,0:T(8,128)(2,1)}), bf16[8,1024,512]{2,1,0:T(8,128)(2,1)}, u32[]{:S(2)}, u32[]{:S(2)}) %all-to-all-start.1) | async-done | bytes 8388640 | tf_op jit(solution)/shard_map/all_to_all | solution.py:50
  574.2 21.9 %gather_fusion.1 = bf16[4096,512]{1,0:T(8,128)(2,1)} fusion(bf16[8192,512]{1,0:T(8,128)(2,1)} %bitcast.7, s32[4096]{0:T(1024)S(1)} %broadcast_clamp_fusion.3), kind=kCustom, calls=%fused_computation.1 | custom fusion | bytes 8404992 | tf_op jit(solution)/shard_map/gather | solution.py:58
  599.3 10.3 %pmax.28 = f32[16,256]{1,0:T(8,128)S(1)} all-reduce(f32[16,256]{1,0:T(8,128)S(1)} %fusion.10), channel_id=1, replica_groups=mesh['docs'=8,'topics'=4] {'topics'}, use_global_device_ids=true, to_apply=%region_5.6 | all-reduce | flops 4096 | bytes 32768 | tf_op jit(solution)/shard_map/pmax | solution.py:24
  609.6 3.7 fusion.32
  613.3 10.1 %psum.28 = f32[16,256]{1,0:T(8,128)S(1)} all-reduce(f32[16,256]{1,0:T(8,128)S(1)} %fusion.32), channel_id=1, replica_groups=mesh['docs'=8,'topics'=4] {'topics'}, use_global_device_ids=true, to_apply=%region_7.8 | all-reduce | flops 4096 | bytes 32768 | tf_op jit(solution)/shard_map/psum | solution.py:25
  623.4 8.1 fusion.34
  632.6 10.1 %pmax.29 = f32[16,256]{1,0:T(8,128)S(1)} all-reduce(f32[16,256]{1,0:T(8,128)S(1)} %fusion.13), channel_id=1, replica_groups=mesh['docs'=8,'topics'=4] {'topics'}, use_global_device_ids=true, to_apply=%region_9.10 | all-reduce | flops 4096 | bytes 32768 | tf_op jit(solution)/shard_map/pmax | solution.py:24
  642.8 3.7 fusion.27
  646.4 10.5 %psum.29 = f32[16,256]{1,0:T(8,128)S(1)} all-reduce(f32[16,256]{1,0:T(8,128)S(1)} %fusion.27), channel_id=1, replica_groups=mesh['docs'=8,'topics'=4] {'topics'}, use_global_device_ids=true, to_apply=%region_11.12 | all-reduce | flops 4096 | bytes 32768 | tf_op jit(solution)/shard_map/psum | solution.py:25
  657.0 8.1 fusion.29
  666.2 10.1 %pmax.30 = f32[16,256]{1,0:T(8,128)S(1)} all-reduce(f32[16,256]{1,0:T(8,128)S(1)} %fusion.16), channel_id=1, replica_groups=mesh['docs'=8,'topics'=4] {'topics'}, use_global_device_ids=true, to_apply=%region_13.14 | all-reduce | flops 4096 | bytes 32768 | tf_op jit(solution)/shard_map/pmax | solution.py:24
  676.3 3.7 fusion.22
  680.0 10.3 %psum.30 = f32[16,256]{1,0:T(8,128)S(1)} all-reduce(f32[16,256]{1,0:T(8,128)S(1)} %fusion.22), channel_id=1, replica_groups=mesh['docs'=8,'topics'=4] {'topics'}, use_global_device_ids=true, to_apply=%region_15.16 | all-reduce | flops 4096 | bytes 32768 | tf_op jit(solution)/shard_map/psum | solution.py:25
  690.3 8.1 fusion.24
  700.1 30.8 %all_gather.3 = f32[128,512]{1,0:T(8,128)S(1)} all-gather(f32[16,512]{1,0:T(8,128)S(1)} %get-tuple-element.4), channel_id=1, replica_groups=mesh['docs'=8,'topics'=4] {'docs'}, dimensions={0}, use_global_device_ids=true | all-gather | bytes 294912 | tf_op jit(solution)/shard_map/all_gather | solution.py:70
  730.9 10.1 %pmax.31 = f32[16,256]{1,0:T(8,128)S(1)} all-reduce(f32[16,256]{1,0:T(8,128)S(1)} %fusion.18), channel_id=1, replica_groups=mesh['docs'=8,'topics'=4] {'topics'}, use_global_device_ids=true, to_apply=%region_19.20 | all-reduce | flops 4096 | bytes 32768 | tf_op jit(solution)/shard_map/pmax | solution.py:24
  741.0 3.7 fusion.20
  744.7 10.1 %psum.31 = f32[16,256]{1,0:T(8,128)S(1)} all-reduce(f32[16,256]{1,0:T(8,128)S(1)} %fusion.20), channel_id=1, replica_groups=mesh['docs'=8,'topics'=4] {'topics'}, use_global_device_ids=true, to_apply=%region_21.22 | all-reduce | flops 4096 | bytes 32768 | tf_op jit(solution)/shard_map/psum | solution.py:25
  754.8 16.1 %scatter_custom_fusion.3 = f32[8192]{0:T(1024)} fusion(s32[4096]{0:T(1024)S(1)} %bitcast.91, f32[4096]{0:T(1024)S(1)} %bitcast.100, f32[]{:T(128)} %constant.31.clone.1), kind=kCustom, calls=%fused_computation.92 | custom fusion | bytes 32772 | tf_op jit(solution)/shard_map/scatter | solution.py:74
  774.5 32.6 %gather_fusion.2 = f32[8192,512]{1,0:T(8,128)} fusion(f32[128,512]{1,0:T(8,128)S(1)} %all_gather.3, s32[8192]{0:T(1024)S(1)} %broadcast_clamp_fusion.1), kind=kCustom, calls=%fused_computation.2 | custom fusion | bytes 33587200 | tf_op jit(solution)/shard_map/gather | solution.py:79
  807.1 13.9 %convert_add_fusion = f32[8,1024,512]{2,1,0:T(8,128)} fusion(f32[8,1024,512]{2,1,0:T(8,128)} %bitcast.80, bf16[8,1024,512]{2,1,0:T(8,128)(2,1)} %bitcast.79), kind=kLoop, calls=%fused_computation.15 | loop fusion | flops 8388608 | bytes 41943040 | tf_op jit(solution)/shard_map/add | solution.py:79
  821.0 11.9 %fusion.7 = f32[8192,512]{1,0:T(8,128)} fusion(f32[8,1024,512]{2,1,0:T(8,128)} %convert_add_fusion, f32[8192]{0:T(1024)S(1)} %bitcast.86, f32[8192]{0:T(1024)S(1)} %bitcast.85), kind=kLoop, calls=%fused_computation.14 | loop fusion | flops 8388608 | bytes 33619968 | tf_op jit(solution)/shard_map/mul | solution.py:80
  832.9 140.0 %scatter_custom_fusion.4 = f32[32768,512]{1,0:T(8,128)} fusion(s32[8192]{0:T(1024)S(1)} %get-tuple-element.2, f32[]{:T(128)} %constant.31.clone.1, f32[8192,512]{1,0:T(8,128)} %fusion.7, s32[8192]{0:T(1024)S(1)} %broadcast_clamp_fusion), kind=kCustom, calls=%fused_computation.9 | custom fusion | flops 4194304 | bytes 67109376 | tf_op jit(solution)/shard_map/scatter-add | solution.py:86
  (54 shorter events, 17.9 us)
Async XLA Ops:
  19.4 40.2 %all-to-all-start = ((s32[8,1,1024]{2,1,0:T(1,128)}), s32[8,1,1024]{2,1,0:T(1,128)S(1)}, u32[]{:S(2)}, u32[]{:S(2)}) async-start(s32[8,1,1024]{2,1,0:T(1,128)} %bitcast.3), calls=%async_computation | async-start | bytes 65536 | tf_op jit(solution)/shard_map/all_to_all | solution.py:45
  59.6 12.7 %all-to-all-start.2 = ((s32[8,1,1024]{2,1,0:T(1,128)}), s32[8,1,1024]{2,1,0:T(1,128)S(1)}, u32[]{:S(2)}, u32[]{:S(2)}) async-start(s32[8,1,1024]{2,1,0:T(1,128)} %bitcast.15), calls=%async_computation.2 | async-start | bytes 65536 | tf_op jit(solution)/shard_map/all_to_all | solution.py:47
  72.3 195.1 %all-to-all-start.3 = ((s32[8,1,1024]{2,1,0:T(1,128)}), s32[8,1,1024]{2,1,0:T(1,128)S(1)}, u32[]{:S(2)}, u32[]{:S(2)}) async-start(s32[8,1,1024]{2,1,0:T(1,128)} %bitcast.17), calls=%async_computation.3 | async-start | bytes 65536 | tf_op jit(solution)/shard_map/all_to_all | solution.py:46
  267.4 124.4 %copy-start.3 = (s32[16,256]{1,0:T(8,128)S(1)}, s32[16,256]{1,0:T(8,128)}, u32[]{:S(2)}) copy-start(s32[16,256]{1,0:T(8,128)} %param.11) | copy-start | bytes 49156
  267.4 124.4 %copy-start.4 = (f32[16,512]{1,0:T(8,128)S(1)}, f32[16,512]{1,0:T(8,128)}, u32[]{:S(2)}) copy-start(f32[16,512]{1,0:T(8,128)} %param.7) | copy-start | bytes 98308
  267.4 306.8 %all-to-all-start.1 = ((bf16[8,1024,512]{2,1,0:T(8,128)(2,1)}), bf16[8,1024,512]{2,1,0:T(8,128)(2,1)}, u32[]{:S(2)}, u32[]{:S(2)}) async-start(bf16[8,1024,512]{2,1,0:T(8,128)(2,1)} %bitcast.78), calls=%async_computation.1 | async-start | bytes 16777216 | tf_op jit(solution)/shard_map/all_to_all | solution.py:50
  596.2 35.3 %copy-start.5 = (f32[512]{0:T(512)S(1)}, f32[512]{0:T(512)}, u32[]{:S(2)}) copy-start(f32[512]{0:T(512)} %param.8) | copy-start | bytes 6148
  623.4 8.3 copy-start
  657.0 8.3 copy-start.1
  690.3 8.9 copy-start.2
  770.9 50.1 %all-to-all-start.4 = ((f32[8,1,1024]{2,1,0:T(1,128)}), f32[8,1,1024]{2,1,0:T(1,128)S(1)}, u32[]{:S(2)}, u32[]{:S(2)}) async-start(f32[8,1,1024]{2,1,0:T(1,128)} %bitcast.23), calls=%async_computation.4 | async-start | bytes 65536 | tf_op jit(solution)/shard_map/all_to_all | solution.py:77
where the time goes:
time: 990 us; the launch traced here: 973 us
  local copies, waits for them, and re-layouts  313 us (32%)
  other arithmetic  195 us (20%)
  waiting for transfers between devices  183 us (18%)
  starting transfers between devices  145 us (15%)
  blocking collectives  113 us (11%)
  matrix products  24.5 us (2%)
    gather x1, local copies, waits for them, and re-layouts, per_device(): found_rows = log_beta[request[0]]  192 us
    all_to_all x1, waiting for transfers between devices, per_device(): lax.all_to_all(found_rows, 'docs', split_axis=0, concat_axis=0, tiled=True)  176 us
    scatter-add x3, other arithmetic, per_device(): sstats = jnp.zeros((log_beta.shape[0], topic_cols), jnp.float32).at[own_r...  146 us
    all_to_all x1, starting transfers between devices, per_device(): lax.all_to_all(found_rows, 'docs', split_axis=0, concat_axis=0, tiled=True)  124 us
    psum x4, blocking collectives, normalized(): lax.psum(jnp.sum(jnp.exp(scores - row_max[:, :, None]), axis=2), 'topics')  41 us
    pmax x4, blocking collectives, normalized(): row_max = lax.pmax(jnp.max(scores, axis=2), 'topics')  40.7 us
    gather x1, local copies, waits for them, and re-layouts, per_device(): rescored = theta_all[source] + found_rows.astype(jnp.float32)  32.6 us
    all_gather x1, blocking collectives, per_device(): theta_all = lax.all_gather(log_theta, 'docs', axis=0, tiled=True)  30.8 us
  transfers between devices with their start and end apart: 5, of which 2 were waited for; matrix products, arithmetic and copies ran while one was open for 29% of the time, Pallas kernels for 0%

commit v1 on v0

v1 whole, which is shorter than its diff:
```python
import jax
import jax.numpy as jnp
from jax import lax
from jax.experimental import pallas as pl
from jax.experimental.pallas import tpu as pltpu
from jax.sharding import PartitionSpec as P

ITERS = 3
COUNT_SPAN = 4
NT = (((1,), (1,)), ((), ()))
TN = (((0,), (0,)), ((), ()))
NN = (((1,), (0,)), ((), ()))


def spread(part, axis):
    size = lax.axis_size(axis)
    return lax.all_to_all(
        jnp.broadcast_to(part[None], (size,) + part.shape), axis, split_axis=0, concat_axis=0, tiled=True
    )


def split_two(values):
    high = values.astype(jnp.bfloat16)
    return high, (values - high.astype(jnp.float32)).astype(jnp.bfloat16)


def dot(left, right, dims):
    return lax.dot_general(left, right, dims, preferred_element_type=jnp.float32)


def params(megabytes=56):
    return pltpu.CompilerParams(
        dimension_semantics=("arbitrary",), vmem_limit_bytes=megabytes * 1024 * 1024
    )


def row_hits(rows, base, extent):
    places = lax.broadcasted_iota(jnp.int32, (extent, rows.shape[1]), 0)
    return jnp.where(places == rows - base, 1.0, 0.0).astype(jnp.bfloat16)


def gather_rows(log_beta, rows, starts, block, chunk):
    vocab, cols = log_beta.shape
    chunks = rows.shape[0]

    def body(starts_ref, rows_ref, beta_ref, out_ref):
        step = pl.program_id(0)

        @pl.when(step == 0)
        def _():
            out_ref[...] = jnp.zeros_like(out_ref)

        low, high = starts_ref[step], starts_ref[step + 1]

        @pl.when(high > low)
        def _():
            def visit(at, carry):
                hits = row_hits(rows_ref[pl.ds(at, 1), :], step * block, block)
                found = dot(hits, beta_ref[...], TN).astype(jnp.bfloat16)
                window = pl.ds(pl.multiple_of(at * chunk, chunk), chunk)
                out_ref[window, :] = out_ref[window, :] + found
                return carry

            lax.fori_loop(low // chunk, (high + chunk - 1) // chunk, visit, 0)

    return pl.pallas_call(
        body,
        grid_spec=pltpu.PrefetchScalarGridSpec(
            num_scalar_prefetch=1,
            grid=(vocab // block,),
            in_specs=[
                pl.BlockSpec((chunks, chunk), lambda i, s: (0, 0)),
                pl.BlockSpec((block, cols), lambda i, s: (i, 0)),
            ],
            out_specs=pl.BlockSpec((chunks * chunk, cols), lambda i, s: (0, 0)),
        ),
        out_shape=jax.ShapeDtypeStruct((chunks * chunk, cols), jnp.bfloat16),
        compiler_params=params(),
        name="gather_rows",
    )(starts, rows, log_beta)


def last_used(used, tile):
    return jnp.maximum((used + tile - 1) // tile - 1, 0)


def shifted_exp(found, used, tile):
    slots, cols = found.shape

    def body(used_ref, found_ref, high_ref, low_ref, top_ref):
        @pl.when(pl.program_id(0) <= last_used(used_ref[0], tile))
        def _():
            values = found_ref[...].astype(jnp.float32)
            top = jnp.max(values, axis=1, keepdims=True)
            high_ref[...], low_ref[...] = split_two(jnp.exp(values - top))
            top_ref[0] = jnp.transpose(jnp.broadcast_to(top, (tile, 128)))[0:1, :]

    def at(i, used):
        return (jnp.minimum(i, last_used(used[0], tile)), 0)

    return pl.pallas_call(
        body,
        grid_spec=pltpu.PrefetchScalarGridSpec(
            num_scalar_prefetch=1,
            grid=(slots // tile,),
            in_specs=[pl.BlockSpec((tile, cols), at)],
            out_specs=[
                pl.BlockSpec((tile, cols), at),
                pl.BlockSpec((tile, cols), at),
                pl.BlockSpec((1, 1, tile), lambda i, used: at(i, used) + (0,)),
            ],
        ),
        out_shape=[
            jax.ShapeDtypeStruct((slots, cols), jnp.bfloat16),
            jax.ShapeDtypeStruct((slots, cols), jnp.bfloat16),
            jax.ShapeDtypeStruct((slots // tile, 1, tile), jnp.float32),
        ],
        compiler_params=params(),
        name="shifted_exp",
    )(used, found)


def slot_mass(theta, beta_high, beta_low, docs, used, tile):
    slots, cols = beta_high.shape
    doc_rows = theta.shape[0]

    def body(used_ref, theta_ref, high_ref, low_ref, docs_ref, mass_ref):
        @pl.when(pl.program_id(0) <= last_used(used_ref[0], tile))
        def _():
            theta_high, theta_low = split_two(theta_ref[...])
            mass = dot(theta_high, high_ref[...], NT)
            mass = mass + dot(theta_low, high_ref[...], NT)
            mass = mass + dot(theta_high, low_ref[...], NT)
            places = lax.broadcasted_iota(jnp.int32, (doc_rows, tile), 0)
            mass_ref[0] = jnp.sum(jnp.where(places == docs_ref[0], mass, 0.0), axis=0, keepdims=True)

    def at(i, used):
        return (jnp.minimum(i, last_used(used[0], tile)), 0)

    def line(i, used):
        return at(i, used) + (0,)

    return pl.pallas_call(
        body,
        grid_spec=pltpu.PrefetchScalarGridSpec(
            num_scalar_prefetch=1,
            grid=(slots // tile,),
            in_specs=[
                pl.BlockSpec((doc_rows, cols), lambda i, used: (0, 0)),
                pl.BlockSpec((tile, cols), at),
                pl.BlockSpec((tile, cols), at),
                pl.BlockSpec((1, 1, tile), line),
            ],
            out_specs=pl.BlockSpec((1, 1, tile), line),
        ),
        out_shape=jax.ShapeDtypeStruct((slots // tile, 1, tile), jnp.float32),
        compiler_params=params(),
        name="slot_mass",
    )(used, theta, beta_high, beta_low, docs)


def doc_sums(weights, docs, beta_high, beta_low, doc_rows, used, tile):
    slots, cols = beta_high.shape

    def body(used_ref, weights_ref, docs_ref, high_ref, low_ref, sums_ref):
        step = pl.program_id(0)

        @pl.when(step == 0)
        def _():
            sums_ref[...] = jnp.zeros_like(sums_ref)

        @pl.when(step <= last_used(used_ref[0], tile))
        def _():
            places = lax.broadcasted_iota(jnp.int32, (doc_rows, tile), 0)
            share_high, share_low = split_two(jnp.where(places == docs_ref[0], weights_ref[0], 0.0))
            sums = dot(share_high, high_ref[...], NN)
            sums = sums + dot(share_low, high_ref[...], NN)
            sums_ref[...] += sums + dot(share_high, low_ref[...], NN)

    def at(i, used):
        return (jnp.minimum(i, last_used(used[0], tile)), 0)

    def line(i, used):
        return at(i, used) + (0,)

    return pl.pallas_call(
        body,
        grid_spec=pltpu.PrefetchScalarGridSpec(
            num_scalar_prefetch=1,
            grid=(slots // tile,),
            in_specs=[
                pl.BlockSpec((1, 1, tile), line),
                pl.BlockSpec((1, 1, tile), line),
                pl.BlockSpec((tile, cols), at),
                pl.BlockSpec((tile, cols), at),
            ],
            out_specs=pl.BlockSpec((doc_rows, cols), lambda i, used: (0, 0)),
        ),
        out_shape=jax.ShapeDtypeStruct((doc_rows, cols), jnp.float32),
        compiler_params=params(),
        name="doc_sums",
    )(used, weights, docs, beta_high, beta_low)


def word_sums(theta, weights, docs, rows, beta_high, beta_low, starts, vocab, block, chunk):
    slots, cols = beta_high.shape
    doc_rows = theta.shape[0]
    chunks = slots // chunk

    def body(starts_ref, theta_ref, weights_ref, docs_ref, rows_ref, high_ref, low_ref, out_ref):
        step = pl.program_id(0)
        out_ref[...] = jnp.zeros_like(out_ref)
        low, high = starts_ref[step], starts_ref[step + 1]

        @pl.when(high > low)
        def _():
            theta_high, theta_low = split_two(theta_ref[...])

            def visit(at, carry):
                window = pl.ds(pl.multiple_of(at * chunk, chunk), chunk)
                line = pl.ds(at, 1)
                places = lax.broadcasted_iota(jnp.int32, (doc_rows, chunk), 0)
                scale_high, scale_low = split_two(
                    jnp.where(places == docs_ref[line, :], weights_ref[line, :], 0.0)
                )
                scaled = dot(scale_high, theta_high, TN)
                scaled = scaled + dot(scale_low, theta_high, TN)
                scaled = scaled + dot(scale_high, theta_low, TN)
                beta = high_ref[window, :].astype(jnp.float32) + low_ref[window, :].astype(jnp.float32)
                term_high, term_low = split_two(scaled * beta)
                hits = row_hits(rows_ref[line, :], step * block, block)
                out_ref[...] += dot(hits, term_high, NN) + dot(hits, term_low, NN)
                return carry

            lax.fori_loop(low // chunk, (high + chunk - 1) // chunk, visit, 0)

    def whole(shape):
        return pl.BlockSpec(shape, lambda i, s: (0, 0), pipeline_mode=pl.Buffered(1))

    return pl.pallas_call(
        body,
        grid_spec=pltpu.PrefetchScalarGridSpec(
            num_scalar_prefetch=1,
            grid=(vocab // block,),
            in_specs=[
                whole((doc_rows, cols)),
                whole((chunks, chunk)),
                whole((chunks, chunk)),
                whole((chunks, chunk)),
                whole((slots, cols)),
                whole((slots, cols)),
            ],
            out_specs=pl.BlockSpec((block, cols), lambda i, s: (i, 0)),
        ),
        out_shape=jax.ShapeDtypeStruct((vocab, cols), jnp.float32),
        compiler_params=params(),
        name="word_sums",
    )(starts, theta, weights, docs, rows, beta_high, beta_low)


def per_device(log_beta, gamma_init, topic_prior, word_block, word_row, counts):
    doc_rows, length = counts.shape
    vocab, cols = log_beta.shape
    owners = lax.axis_size("docs")
    tokens = doc_rows * length
    slots = 2 * tokens
    all_docs = owners * doc_rows
    block = min(512, vocab)
    chunk = min(256, slots)
    tile = min(1024, slots)

    sent = jnp.stack([word_block[:, :, 0] * vocab + word_row, counts])
    named = spread(sent, "docs")
    row = named[:, 0] - lax.axis_index("docs") * vocab
    count = named[:, 1]
    doc = (
        lax.broadcasted_iota(jnp.int32, row.shape, 0) * doc_rows
        + lax.broadcasted_iota(jnp.int32, row.shape, 1)
    )
    code = (row * all_docs + doc) * COUNT_SPAN + count
    none = jnp.int32(vocab * all_docs * COUNT_SPAN)
    mine = (row >= 0) & (row < vocab) & (count > 0)
    code = jnp.sort(jnp.where(mine, code, none).reshape(-1))[:slots]
    filled = code < none
    slot_count = jnp.where(filled, code % COUNT_SPAN, 0).astype(jnp.float32)
    slot_doc = jnp.where(filled, code // COUNT_SPAN % all_docs, all_docs)
    slot_row = code // (COUNT_SPAN * all_docs)
    bounds = jnp.arange(vocab // block + 1, dtype=jnp.int32) * (block * all_docs * COUNT_SPAN)
    starts = jnp.sum((code[None, :] < bounds[:, None]).astype(jnp.int32), axis=1)
    used = starts[-1:]
    lines = (slots // tile, 1, tile)
    rows2 = slot_row.reshape(slots // chunk, chunk)
    docs3 = slot_doc.reshape(lines)
    count3 = slot_count.reshape(lines)

    found = gather_rows(log_beta, rows2, starts, block, chunk)
    beta_high, beta_low, top = shifted_exp(found, used, tile)

    gamma = gamma_init
    for sweep in range(ITERS + 1):
        theta = jnp.exp(lax.digamma(gamma))
        theta_all = spread(theta, "docs").reshape(all_docs, cols)
        mass = slot_mass(theta_all, beta_high, beta_low, docs3, used, tile)
        if sweep == 0:
            pairs = spread(jnp.stack([top, mass]), "topics")
            tops = jnp.max(pairs[:, 0], axis=0)
            factor = jnp.exp(top - tops)
            total = jnp.sum(pairs[:, 1] * jnp.exp(pairs[:, 0] - tops[None]), axis=0)
        else:
            total = jnp.sum(spread(mass * factor, "topics"), axis=0)
        weights = jnp.where(count3 > 0, count3 * factor / total, 0.0)
        if sweep < ITERS:
            sums = doc_sums(weights, docs3, beta_high, beta_low, all_docs, used, tile)
            sums = lax.all_to_all(
                sums.reshape(owners, doc_rows, cols), "docs", split_axis=0, concat_axis=0, tiled=True
            )
            gamma = topic_prior[None, :] + theta * jnp.sum(sums, axis=0)
    sstats = word_sums(
        theta_all,
        weights.reshape(slots // chunk, chunk),
        slot_doc.reshape(slots // chunk, chunk),
        rows2,
        beta_high,
        beta_low,
        starts,
        vocab,
        block,
        chunk,
    )
    return (gamma, sstats)


def solution(mesh):
    in_specs = (
        P("docs", "topics"),
        P("docs", "topics"),
        P("topics"),
        P("docs", None, None),
        P("docs", None),
        P("docs", None),
    )
    out_specs = (P("docs", "topics"), P("docs", "topics"))
    return jax.shard_map(
        per_device, mesh=mesh, in_specs=in_specs, out_specs=out_specs, check_vma=False
    )
```

time: 990 us -> 358 us (0.36); the launches traced: 973 us -> 358 us
  local copies, waits for them, and re-layouts: 313 us -> 6.38 us
  Pallas kernels: 0 us -> 210 us
  other arithmetic: 195 us -> 19.7 us
  waiting for transfers between devices: 183 us -> 7.74 us
  starting transfers between devices: 145 us -> 10.9 us
  matrix products: 24.5 us -> 0 us
  blocking collectives: 113 us -> 102 us
    gather x3 -> x0, local copies, waits for them, and re-layouts: 246 us -> none  [the longest x1 192 us: per_device(): found_rows = log_beta[request[0]]]
    pallas_call x0 -> x10, Pallas kernels: none -> 210 us  [the longest x1 81.7 us: word_sums(): pl.pallas_call(body, grid_spec=pltpu.PrefetchScalarGridSpec(num_scalar_pr...]
    all_to_all x5 -> x2, waiting for transfers between devices: 183 us -> 7.74 us  [spread(): lax.all_to_all(jnp.broadcast_to(part[None], (size,) + part.shape), axis,...]
    scatter-add x3 -> x0, other arithmetic: 146 us -> none  [per_device(): sstats = jnp.zeros((log_beta.shape[0], topic_cols), jnp.float32).at[own_r...]
    all_to_all x5 -> x2, starting transfers between devices: 145 us -> 10.9 us  [spread(): lax.all_to_all(jnp.broadcast_to(part[None], (size,) + part.shape), axis,...]
    all_to_all x0 -> x10, blocking collectives: none -> 102 us  [the longest x7 65.8 us: spread(): lax.all_to_all(jnp.broadcast_to(part[None], (size,) + part.shape), axis,...]
    scatter x4 -> x0, local copies, waits for them, and re-layouts: 64.4 us -> none  [the longest x1 16.1 us: per_device(): blank_ids.at[places].set(word_row.reshape(tokens)).reshape(owners, capacity)]
    psum x4 -> x0, blocking collectives: 41 us -> none  [normalized(): lax.psum(jnp.sum(jnp.exp(scores - row_max[:, :, None]), axis=2), 'topics')]
  transfers between devices with their start and end apart: 5 -> 2, of which waited for: 2 -> 1; matrix products, arithmetic and copies ran while one was open for 29% -> 4% of each run, Pallas kernels for 0% -> 18%
where the time goes in v1:
time: 358 us
  Pallas kernels  210 us (59%)
  blocking collectives  102 us (28%)
  other arithmetic  19.7 us (6%)
  starting transfers between devices  10.9 us (3%)
  waiting for transfers between devices  7.74 us (2%)
  local copies, waits for them, and re-layouts  6.38 us (2%)
    pallas_call x1, Pallas kernels, word_sums(): pl.pallas_call(body, grid_spec=pltpu.PrefetchScalarGridSpec(num_scalar_pr...  81.7 us
    all_to_all x7, blocking collectives, spread(): lax.all_to_all(jnp.broadcast_to(part[None], (size,) + part.shape), axis,...  65.8 us
    pallas_call x1, Pallas kernels, gather_rows(): pl.pallas_call(body, grid_spec=pltpu.PrefetchScalarGridSpec(num_scalar_pr...  54.1 us
    pallas_call x4, Pallas kernels, slot_mass(): pl.pallas_call(body, grid_spec=pltpu.PrefetchScalarGridSpec(num_scalar_pr...  40.1 us
    all_to_all x3, blocking collectives, per_device(): lax.all_to_all(sums.reshape(owners, doc_rows, cols), 'docs', split_axis=0...  36.5 us
    pallas_call x3, Pallas kernels, doc_sums(): pl.pallas_call(body, grid_spec=pltpu.PrefetchScalarGridSpec(num_scalar_pr...  24.8 us
    sort x1, other arithmetic, per_device(): code = jnp.sort(jnp.where(mine, code, none).reshape(-1))[:slots]  11.2 us
    all_to_all x2, starting transfers between devices, spread(): lax.all_to_all(jnp.broadcast_to(part[None], (size,) + part.shape), axis,...  10.9 us
  transfers between devices with their start and end apart: 2, of which 1 were waited for; matrix products, arithmetic and copies ran while one was open for 4% of the time, Pallas kernels for 18%

profile of v1, /device:TPU:0, one launch (start us, length us, event | category | flops | bytes accessed | tf_op | source)
XLA Modules:
  0.0 358.3 jit_solution(16151998648524735924)
XLA Ops:
  0.6 0.7 fusion.41
  2.1 0.7 broadcast_in_dim.38
  2.8 7.3 %all-to-all-start = ((s32[8,2,16,256]{3,2,1,0:T(8,128)}), s32[8,2,16,256]{3,2,1,0:T(8,128)S(1)}, u32[]{:S(2)}, u32[]{:S(2)}) async-start(s32[8,2,16,256]{3,2,1,0:T(8,128)} %broadcast_in_dim.38), calls=%async_computation | async-start | bytes 524288 | tf_op jit(solution)/shard_map/all_to_all | solution.py:17
  10.3 1.0 fusion.7
  11.3 7.7 %all-to-all-done = s32[8,2,16,256]{3,2,1,0:T(8,128)S(1)} async-done(((s32[8,2,16,256]{3,2,1,0:T(8,128)}), s32[8,2,16,256]{3,2,1,0:T(8,128)S(1)}, u32[]{:S(2)}, u32[]{:S(2)}) %all-to-all-start) | async-done | bytes 262176 | tf_op jit(solution)/shard_map/all_to_all | solution.py:17
  19.7 3.6 %all-to-all-start.1 = ((f32[8,16,512]{2,1,0:T(8,128)}), f32[8,16,512]{2,1,0:T(8,128)S(1)}, u32[]{:S(2)}, u32[]{:S(2)}) async-start(f32[8,16,512]{2,1,0:T(8,128)} %broadcast_in_dim.40), calls=%async_computation.1 | async-start | bytes 524288 | tf_op jit(solution)/shard_map/all_to_all | solution.py:17
  23.7 11.2 %sort.15 = (s32[32768]{0:T(1024)S(1)}, s32[32768]{0:T(1024)}) sort(s32[32768]{0:T(1024)S(1)} %add_select_fusion, s32[32768]{0:T(1024)S(1)} %iota.24), dimensions={0}, to_apply=%region_0.1 | sort | flops 491520 | bytes 524288 | tf_op jit(solution)/shard_map/jit(sort)/sort | solution.py:283
  37.2 54.1 %gather_rows.1.found_ref = bf16[8192,512]{1,0:T(8,128)(2,1)} custom-call(s32[65]{0:T(128)} %copy-done.4, s32[32,256]{1,0:T(8,128)} %get-tuple-element.20.rows_ref, bf16[32768,512]{1,0:T(8,128)(2,1)} %beta_ref.1), custom_call_target="tpu_custom_call" | custom-call | tf_op jit(solution)/shard_map/gather_rows/pallas_call | solution.py:66
  91.4 9.8 %shifted_exp.1 = (bf16[8192,512]{1,0:T(8,128)(2,1)}, bf16[8192,512]{1,0:T(8,128)(2,1)}, f32[8,1,1024]{2,1,0:T(1,128)}) custom-call(s32[1]{0:T(128)} %slice.64.used_ref, bf16[8192,512]{1,0:T(8,128)(2,1)} %gather_rows.1.found_ref), custom_call_target="tpu_custom_call" | custom-call | tf_op jit(solution)/shard_map/shifted_exp/pallas_call | solution.py:101
  101.9 10.0 %slot_mass.4 = f32[8,1,1024]{2,1,0:T(1,128)} custom-call(s32[1]{0:T(128)} %slice.64.used_ref, f32[128,512]{1,0:T(8,128)} %bitcast.88, bf16[8192,512]{1,0:T(8,128)(2,1)} %get-tuple-element.9.high_ref, bf16[8192,512]{1,0:T(8,128)(2,1)} %get-tuple-element.10.low_ref, s32[8,1,1024]{2,1,0:T(1,128)} %select_n.75.docs_ref), custom_call_target="tpu_custom_call" | custom-call | tf_op jit(solution)/shard_map/slot_mass/pallas_call | solution.py:143
  111.9 0.8 pad_maximum_fusion
  112.8 8.6 %all_to_all.60 = f32[4,2,8,1,1024]{4,2,3,1,0:T(8,128)S(1)} all-to-all(f32[4,2,8,1,1024]{4,2,3,1,0:T(8,128)S(1)} %broadcast_in_dim.42), channel_id=1, replica_groups=mesh['docs'=8,'topics'=4] {'topics'}, dimensions={0} | all-to-all | bytes 524288 | tf_op jit(solution)/shard_map/all_to_all | solution.py:17
  122.1 8.3 %doc_sums.3 = f32[128,512]{1,0:T(8,128)} custom-call(s32[1]{0:T(128)} %slice.64.used_ref, f32[8,1,1024]{2,1,0:T(1,128)} %copy.31.weights_ref, s32[8,1,1024]{2,1,0:T(1,128)} %select_n.75.docs_ref, bf16[8192,512]{1,0:T(8,128)(2,1)} %get-tuple-element.9.high_ref, bf16[8192,512]{1,0:T(8,128)(2,1)} %get-tuple-element.10.low_ref), custom_call_target="tpu_custom_call" | custom-call | tf_op jit(solution)/shard_map/doc_sums/pallas_call | solution.py:186
  130.4 12.2 %all_to_all.61 = f32[8,16,512]{2,1,0:T(8,128)S(1)} all-to-all(f32[8,16,512]{2,1,0:T(8,128)} %bitcast.89), channel_id=1, replica_groups=mesh['docs'=8,'topics'=4] {'docs'}, dimensions={0} | all-to-all | bytes 524288 | tf_op jit(solution)/shard_map/all_to_all | solution.py:314
  143.1 12.1 %all_to_all.62 = f32[8,16,512]{2,1,0:T(8,128)} all-to-all(f32[8,16,512]{2,1,0:T(8,128)S(1)} %broadcast_in_dim.43), channel_id=1, replica_groups=mesh['docs'=8,'topics'=4] {'docs'}, dimensions={0} | all-to-all | bytes 524288 | tf_op jit(solution)/shard_map/all_to_all | solution.py:17
  155.2 10.0 %slot_mass.5 = f32[8,1,1024]{2,1,0:T(1,128)} custom-call(s32[1]{0:T(128)} %slice.64.used_ref, f32[128,512]{1,0:T(8,128)} %bitcast.90, bf16[8192,512]{1,0:T(8,128)(2,1)} %get-tuple-element.9.high_ref, bf16[8192,512]{1,0:T(8,128)(2,1)} %get-tuple-element.10.low_ref, s32[8,1,1024]{2,1,0:T(1,128)} %select_n.75.docs_ref), custom_call_target="tpu_custom_call" | custom-call | tf_op jit(solution)/shard_map/slot_mass/pallas_call | solution.py:143
  165.2 0.8 fusion.32
  166.0 7.0 %all_to_all.63 = f32[4,8,1,1024]{3,1,2,0:T(8,128)S(1)} all-to-all(f32[4,8,1,1024]{3,1,2,0:T(8,128)S(1)} %broadcast_in_dim.45), channel_id=1, replica_groups=mesh['docs'=8,'topics'=4] {'topics'}, dimensions={0} | all-to-all | bytes 262144 | tf_op jit(solution)/shard_map/all_to_all | solution.py:17
  173.6 8.3 %doc_sums.4 = f32[128,512]{1,0:T(8,128)} custom-call(s32[1]{0:T(128)} %slice.64.used_ref, f32[8,1,1024]{2,1,0:T(1,128)} %copy.33.weights_ref, s32[8,1,1024]{2,1,0:T(1,128)} %select_n.75.docs_ref, bf16[8192,512]{1,0:T(8,128)(2,1)} %get-tuple-element.9.high_ref, bf16[8192,512]{1,0:T(8,128)(2,1)} %get-tuple-element.10.low_ref), custom_call_target="tpu_custom_call" | custom-call | tf_op jit(solution)/shard_map/doc_sums/pallas_call | solution.py:186
  181.9 12.2 %all_to_all.64 = f32[8,16,512]{2,1,0:T(8,128)S(1)} all-to-all(f32[8,16,512]{2,1,0:T(8,128)} %bitcast.91), channel_id=1, replica_groups=mesh['docs'=8,'topics'=4] {'docs'}, dimensions={0} | all-to-all | bytes 524288 | tf_op jit(solution)/shard_map/all_to_all | solution.py:314
  194.4 12.1 %all_to_all.65 = f32[8,16,512]{2,1,0:T(8,128)} all-to-all(f32[8,16,512]{2,1,0:T(8,128)S(1)} %broadcast_in_dim.46), channel_id=1, replica_groups=mesh['docs'=8,'topics'=4] {'docs'}, dimensions={0} | all-to-all | bytes 524288 | tf_op jit(solution)/shard_map/all_to_all | solution.py:17
  206.4 10.0 %slot_mass.6 = f32[8,1,1024]{2,1,0:T(1,128)} custom-call(s32[1]{0:T(128)} %slice.64.used_ref, f32[128,512]{1,0:T(8,128)} %bitcast.92, bf16[8192,512]{1,0:T(8,128)(2,1)} %get-tuple-element.9.high_ref, bf16[8192,512]{1,0:T(8,128)(2,1)} %get-tuple-element.10.low_ref, s32[8,1,1024]{2,1,0:T(1,128)} %select_n.75.docs_ref), custom_call_target="tpu_custom_call" | custom-call | tf_op jit(solution)/shard_map/slot_mass/pallas_call | solution.py:143
  216.4 0.8 fusion.31
  217.2 7.0 %all_to_all.66 = f32[4,8,1,1024]{3,1,2,0:T(8,128)S(1)} all-to-all(f32[4,8,1,1024]{3,1,2,0:T(8,128)S(1)} %broadcast_in_dim.90), channel_id=1, replica_groups=mesh['docs'=8,'topics'=4] {'topics'}, dimensions={0} | all-to-all | bytes 262144 | tf_op jit(solution)/shard_map/all_to_all | solution.py:17
  224.9 8.3 %doc_sums.5 = f32[128,512]{1,0:T(8,128)} custom-call(s32[1]{0:T(128)} %slice.64.used_ref, f32[8,1,1024]{2,1,0:T(1,128)} %copy.35.weights_ref, s32[8,1,1024]{2,1,0:T(1,128)} %select_n.75.docs_ref, bf16[8192,512]{1,0:T(8,128)(2,1)} %get-tuple-element.9.high_ref, bf16[8192,512]{1,0:T(8,128)(2,1)} %get-tuple-element.10.low_ref), custom_call_target="tpu_custom_call" | custom-call | tf_op jit(solution)/shard_map/doc_sums/pallas_call | solution.py:186
  233.2 12.2 %all_to_all.67 = f32[8,16,512]{2,1,0:T(8,128)S(1)} all-to-all(f32[8,16,512]{2,1,0:T(8,128)} %bitcast.93), channel_id=1, replica_groups=mesh['docs'=8,'topics'=4] {'docs'}, dimensions={0} | all-to-all | bytes 524288 | tf_op jit(solution)/shard_map/all_to_all | solution.py:314
  245.3 0.7 fusion.21
  246.1 12.1 %all_to_all.68 = f32[8,16,512]{2,1,0:T(8,128)} all-to-all(f32[8,16,512]{2,1,0:T(8,128)S(1)} %broadcast_in_dim.91), channel_id=1, replica_groups=mesh['docs'=8,'topics'=4] {'docs'}, dimensions={0} | all-to-all | bytes 524288 | tf_op jit(solution)/shard_map/all_to_all | solution.py:17
  258.2 10.0 %slot_mass.7 = f32[8,1,1024]{2,1,0:T(1,128)} custom-call(s32[1]{0:T(128)} %slice.64.used_ref, f32[128,512]{1,0:T(8,128)} %bitcast.86, bf16[8192,512]{1,0:T(8,128)(2,1)} %get-tuple-element.9.high_ref, bf16[8192,512]{1,0:T(8,128)(2,1)} %get-tuple-element.10.low_ref, s32[8,1,1024]{2,1,0:T(1,128)} %select_n.75.docs_ref), custom_call_target="tpu_custom_call" | custom-call | tf_op jit(solution)/shard_map/slot_mass/pallas_call | solution.py:143
  268.2 0.8 fusion.30
  269.0 7.0 %all_to_all.69 = f32[4,8,1,1024]{3,1,2,0:T(8,128)S(1)} all-to-all(f32[4,8,1,1024]{3,1,2,0:T(8,128)S(1)} %broadcast_in_dim.93), channel_id=1, replica_groups=mesh['docs'=8,'topics'=4] {'topics'}, dimensions={0} | all-to-all | bytes 262144 | tf_op jit(solution)/shard_map/all_to_all | solution.py:17
  276.6 81.7 %word_sums.1 = f32[32768,512]{1,0:T(8,128)} custom-call(s32[65]{0:T(128)} %copy-done.4, f32[128,512]{1,0:T(8,128)} %bitcast.87, f32[32,256]{1,0:T(8,128)} %reshape.205.weights_ref, s32[32,256]{1,0:T(8,128)} %get-tuple-element.19.docs_ref, s32[32,256]{1,0:T(8,128)} %get-tuple-element.20.rows_ref, bf16[8192,512]{1,0:T(8,128)(2,1)} %get-tuple-element.9.high_ref, ...), custom_call_target="tpu_custom_call" | custom-call | tf_op jit(solution)/shard_map/word_sums/pallas_call | solution.py:240
  (58 shorter events, 8.6 us)
Async XLA Ops:
  2.8 16.2 %all-to-all-start = ((s32[8,2,16,256]{3,2,1,0:T(8,128)}), s32[8,2,16,256]{3,2,1,0:T(8,128)S(1)}, u32[]{:S(2)}, u32[]{:S(2)}) async-start(s32[8,2,16,256]{3,2,1,0:T(8,128)} %broadcast_in_dim.38), calls=%async_computation | async-start | bytes 524288 | tf_op jit(solution)/shard_map/all_to_all | solution.py:17
  19.7 81.4 %all-to-all-start.1 = ((f32[8,16,512]{2,1,0:T(8,128)}), f32[8,16,512]{2,1,0:T(8,128)S(1)}, u32[]{:S(2)}, u32[]{:S(2)}) async-start(f32[8,16,512]{2,1,0:T(8,128)} %broadcast_in_dim.40), calls=%async_computation.1 | async-start | bytes 524288 | tf_op jit(solution)/shard_map/all_to_all | solution.py:17
  35.3 2.0 copy-start.4
  101.2 0.7 copy-start
  101.9 10.0 %copy-start.1 = (f32[8,1,1024]{2,1,0:T(1,128)S(1)}, f32[8,1,1024]{2,1,0:T(1,128)}, u32[]{:S(2)}) copy-start(f32[8,1,1024]{2,1,0:T(1,128)} %get-tuple-element.8) | copy-start | bytes 98308
  122.1 20.4 %copy-start.2 = (f32[16,512]{1,0:T(8,128)S(1)}, f32[16,512]{1,0:T(8,128)}, u32[]{:S(2)}) copy-start(f32[16,512]{1,0:T(8,128)} %param.7) | copy-start | bytes 98308
  122.1 20.4 %copy-start.3 = (f32[512]{0:T(512)S(1)}, f32[512]{0:T(512)}, u32[]{:S(2)}) copy-start(f32[512]{0:T(512)} %param.8) | copy-start | bytes 6148
